TPU v7x, 32 devices: a whole 2x2x4 slice. The times are simulated.
32 devices in a mesh: row: 4 (over y, x), col: 8 (over z, core).
Axes of the slice: x: 2, y: 2, z: 4, core: 2. Of those that a mesh axis runs over, the one named last changes fastest.
Arguments:
- pair_rep: float32 [64, 64, 128], P('row', 'col'), may hold values from -160 to 160
- ln_gain: float32 [128], replicated, may hold values from 0.25 to 1.75
- ln_bias: float32 [128], replicated, may hold values from -3 to 3
- w_in: float32 [1024, 128], replicated, may hold values from -0.5 to 0.5
- w_out: float32 [512, 128], replicated, may hold values from -0.25 to 0.25
- w_pde: float32 [128, 64], replicated, may hold values from -2 to 2
- labels: int32 [64, 64], P('row', 'col'), may hold values from 0 to 63
- pair_mask: int32 [64, 64], P('row', 'col'), may hold values from 0 to 1, as said below
Outputs:
- mean_loss: float32 [], replicated
- d_pair_rep: float32 [64, 64, 128], P('row', 'col')
- d_ln_gain: float32 [128], replicated
- d_ln_bias: float32 [128], replicated
- d_w_in: float32 [1024, 128], P(('row', 'col'))
- d_w_out: float32 [512, 128], P(('row', 'col'))
- d_w_pde: float32 [128, 64], replicated
Inputs may be any that keep to these rules, and one draw needn't show every extreme that they name: pair_mask[i][j] = m_i m_j for a flag m_i of token i, with m_i = 1 whenever i is a multiple of 16.
All inputs are finite; a program needn't handle non-finite values.
Results may differ from a plain program's by a relative error of at most 0.0003.
Values sent between devices are 32-bit elements; how exact they have to be, the bound alone decides.
A program may use at most 64 MiB of HBM per device.

v0:
```python
import jax
import jax.numpy as jnp
from jax import lax
from jax.sharding import PartitionSpec as P

epsilon = 1e-05


def transition(rows_block, ln_gain, ln_bias, w_in, w_out):
    average = jnp.mean(rows_block, axis=-1, keepdims=True)
    centred = rows_block - average
    variance = jnp.mean(centred * centred, axis=-1, keepdims=True)
    normed = centred * lax.rsqrt(variance + epsilon) * ln_gain + ln_bias
    projected_in = lax.dot_general(
        normed,
        w_in,
        (((1,), (1,)), ((), ())),
        precision=lax.Precision.HIGHEST,
        preferred_element_type=jnp.float32,
    )
    hidden_units = w_out.shape[0]
    hidden = jax.nn.silu(projected_in[:, :hidden_units]) * projected_in[:, hidden_units:]
    return rows_block + jnp.dot(
        hidden, w_out, precision=lax.Precision.HIGHEST, preferred_element_type=jnp.float32
    )


def group_rows(tile_rows, tile_cols):
    stride_rows = 1
    while (
        stride_rows < tile_rows
        and stride_rows * tile_cols < 1024
        and (tile_rows % (stride_rows * 2) == 0)
    ):
        stride_rows = stride_rows * 2
    return stride_rows


def mirror(tile):
    row_devices = lax.axis_size("row")
    col_devices = lax.axis_size("col")
    factor = col_devices // row_devices
    tile_cols = tile.shape[1]
    channels = tile.shape[2]
    slab_rows = tile_cols // row_devices
    pieces = tile.reshape(factor, row_devices, slab_rows, tile_cols * channels)
    pieces = lax.all_to_all(
        lax.all_to_all(pieces, "row", split_axis=1, concat_axis=0, tiled=True),
        "col",
        split_axis=0,
        concat_axis=0,
        tiled=True,
    )
    pieces = pieces.reshape(row_devices, factor, slab_rows, tile_cols * channels)
    pieces = lax.all_to_all(pieces, "row", split_axis=0, concat_axis=2, tiled=True)
    pieces = pieces.reshape(factor, tile_cols, tile_cols, channels)
    return jnp.transpose(pieces, (0, 2, 1, 3)).reshape(factor * tile_cols, tile_cols, channels)


def on_device(pair_rep, ln_gain, ln_bias, w_in, w_out, w_pde, labels, pair_mask):
    tile_rows, tile_cols, channels = pair_rep.shape
    stride_rows = group_rows(tile_rows, tile_cols)
    blocks = pair_rep.reshape(tile_rows // stride_rows, stride_rows * tile_cols, channels)

    def forward(rows_block):
        return transition(rows_block, ln_gain, ln_bias, w_in, w_out)

    updated = lax.map(forward, blocks).reshape(tile_rows, tile_cols, channels)
    mask_float = pair_mask.astype(jnp.float32)
    local_count = jnp.sum(mask_float)
    valid_count = lax.psum(local_count, ("row", "col"))
    inverse_count = 1.0 / valid_count
    projected = jnp.einsum("ijc,cb->ijb", updated, w_pde, precision=lax.Precision.HIGHEST)
    scores = projected + mirror(projected)
    highest = jnp.max(scores, axis=-1, keepdims=True)
    shifted = jnp.exp(scores - highest)
    exp_total = jnp.sum(shifted, axis=-1, keepdims=True)
    log_total = highest + jnp.log(exp_total)
    bin_index = lax.broadcasted_iota(jnp.int32, (1, 1, scores.shape[2]), 2)
    onehot = (labels[:, :, None] == bin_index).astype(jnp.float32)
    picked = jnp.sum(scores * onehot, axis=-1, keepdims=True)
    local_loss = jnp.sum(mask_float * (log_total - picked)[:, :, 0])
    d_scores = mask_float[:, :, None] * (shifted / exp_total - onehot) * inverse_count
    d_sym = d_scores + mirror(d_scores)
    d_updated = jnp.einsum("ijb,cb->ijc", d_sym, w_pde, precision=lax.Precision.HIGHEST)
    grad_pde = jnp.einsum("ijc,ijb->cb", updated, d_sym, precision=lax.Precision.HIGHEST)
    cot_blocks = d_updated.reshape(blocks.shape)

    def backward(totals, pieces):
        rows_block, cotangent = pieces
        outcome, pullback = jax.vjp(transition, rows_block, ln_gain, ln_bias, w_in, w_out)
        gradients = pullback(cotangent)
        merged = tuple((earlier + later for earlier, later in zip(totals, gradients[1:])))
        return (merged, gradients[0])

    start_sums = (
        jnp.zeros_like(ln_gain),
        jnp.zeros_like(ln_bias),
        jnp.zeros_like(w_in),
        jnp.zeros_like(w_out),
    )
    param_sums, d_blocks = lax.scan(backward, start_sums, (blocks, cot_blocks))
    g_gain, g_bias, g_in, g_out = param_sums
    row_in, row_out = (
        lax.psum_scatter(g_in, "row", scatter_dimension=0, tiled=True),
        lax.psum_scatter(g_out, "row", scatter_dimension=0, tiled=True),
    )
    shard_in, shard_out = (
        lax.psum_scatter(row_in, "col", scatter_dimension=0, tiled=True),
        lax.psum_scatter(row_out, "col", scatter_dimension=0, tiled=True),
    )
    loss_sum, gain_sum, bias_sum, pde_sum = lax.psum(
        (local_loss, g_gain, g_bias, grad_pde), ("row", "col")
    )
    late_scale = 1.0
    mean_loss = loss_sum / valid_count
    d_pair_rep = d_blocks.reshape(pair_rep.shape) * late_scale
    return (
        mean_loss,
        d_pair_rep,
        gain_sum * late_scale,
        bias_sum * late_scale,
        shard_in * late_scale,
        shard_out * late_scale,
        pde_sum * late_scale,
    )


def solution(mesh):
    placed = (P("row", "col", None), P(), P(), P(), P(), P(), P("row", "col"), P("row", "col"))
    return jax.shard_map(
        on_device,
        mesh=mesh,
        in_specs=placed,
        out_specs=(
            P(),
            P("row", "col", None),
            P(),
            P(),
            P(("row", "col"), None),
            P(("row", "col"), None),
            P(),
        ),
        check_vma=False,
    )
```

profile of v0, /device:TPU:0, one launch (start us, length us, event | category | flops | bytes accessed | tf_op | source)
XLA Modules:
  0.0 227.3 jit_solution(3535305278162302303)
XLA Ops:
  7.2 1.0 reduce_sum.109
  8.2 0.1 div.52
  8.3 0.2 multiply_reduce_fusion.2
  8.5 0.1 add.95
  8.6 0.6 copy-done.3
  9.2 0.6 fusion.8
  9.9 0.3 copy-done.7
  10.2 0.4 fusion
  10.6 0.3 copy-done.2
  11.0 0.2 fusion.10
  11.2 0.1 reshape.118
  11.3 9.7 %all_to_all.76 = f32[2,4,2,512]{3,2,0,1:T(2,128)S(1)} all-to-all(f32[2,4,2,512]{3,2,0,1:T(2,128)S(1)} %copy.34), channel_id=1, replica_groups=mesh['row'=4,'col'=8] {'row'}, dimensions={1} | all-to-all | bytes 65536 | tf_op jit(solution)/shard_map/all_to_all | solution.py:48
  21.0 10.5 %all_to_all.77 = f32[8,1,2,512]{3,2,1,0:T(2,128)} all-to-all(f32[8,1,2,512]{3,2,1,0:T(2,128)S(1)} %bitcast.70), channel_id=1, replica_groups=mesh['row'=4,'col'=8] {'col'}, dimensions={0} | all-to-all | bytes 65536 | tf_op jit(solution)/shard_map/all_to_all | solution.py:47
  31.5 3.4 %all-to-all-start.2 = ((f32[4,2,2,512]{3,2,1,0:T(2,128)}), f32[4,2,2,512]{3,2,1,0:T(2,128)S(1)}, u32[]{:S(2)}, u32[]{:S(2)}) async-start(f32[4,2,2,512]{3,2,1,0:T(2,128)} %bitcast.7), calls=%async_computation.2 | async-start | bytes 65536 | tf_op jit(solution)/shard_map/all_to_all | solution.py:55
  34.9 0.0 reduce-scatter.9.cloned.1.call-start
  35.0 0.1 copy.38
  35.1 0.5 copy-done.5
  35.6 0.1 copy.33
  35.7 4.0 %all-to-all-done.2 = f32[4,2,2,512]{3,2,1,0:T(2,128)S(1)} async-done(((f32[4,2,2,512]{3,2,1,0:T(2,128)}), f32[4,2,2,512]{3,2,1,0:T(2,128)S(1)}, u32[]{:S(2)}, u32[]{:S(2)}) %all-to-all-start.2) | async-done | bytes 32800 | tf_op jit(solution)/shard_map/all_to_all | solution.py:55
  39.7 0.1 reshape.120
  39.8 0.1 fusion.26
  39.9 0.2 fusion.7
  40.1 0.6 convert_reduce_fusion
  40.7 38.5 %psum.36 = f32[]{:T(128)} all-reduce(f32[]{:T(128)} %get-tuple-element.57), channel_id=1, replica_groups=mesh['row'=4,'col'=8] {'row','col'}, use_global_device_ids=true, to_apply=%region_8.9 | all-reduce | flops 1 | bytes 8 | tf_op jit(solution)/shard_map/psum | solution.py:71
  79.9 0.1 multiply_multiply_fusion
  80.0 0.1 reshape.122
  80.1 8.4 %all_to_all.78 = f32[2,4,2,512]{3,2,0,1:T(2,128)S(1)} all-to-all(f32[2,4,2,512]{3,2,0,1:T(2,128)S(1)} %copy.39), channel_id=1, replica_groups=mesh['row'=4,'col'=8] {'row'}, dimensions={1} | all-to-all | bytes 65536 | tf_op jit(solution)/shard_map/all_to_all | solution.py:48
  88.5 8.4 %all_to_all.79 = f32[8,1,2,512]{3,2,1,0:T(2,128)S(1)} all-to-all(f32[8,1,2,512]{3,2,1,0:T(2,128)S(1)} %bitcast.71), channel_id=1, replica_groups=mesh['row'=4,'col'=8] {'col'}, dimensions={0} | all-to-all | bytes 65536 | tf_op jit(solution)/shard_map/all_to_all | solution.py:47
  96.9 7.1 %all_to_all.80 = f32[4,2,2,512]{3,2,1,0:T(2,128)S(1)} all-to-all(f32[4,2,2,512]{3,2,1,0:T(2,128)S(1)} %bitcast.72), channel_id=1, replica_groups=mesh['row'=4,'col'=8] {'row'}, dimensions={0} | all-to-all | bytes 65536 | tf_op jit(solution)/shard_map/all_to_all | solution.py:55
  104.0 0.1 reshape.124
  104.1 0.1 bitcast_add_fusion
  104.3 0.2 convolution_bitcast_fusion
  104.5 1.3 fusion.6
  105.8 0.0 reduce-scatter.9.cloned.1.call-update
  105.8 0.0 reduce-scatter.5.cloned.1.call-start
  105.9 0.4 fusion.23
  106.3 1.8 fusion.1
  108.2 0.0 reduce-scatter.11.cloned.1.call-start
  108.2 0.7 multiply_reduce_fusion
  108.9 0.2 fusion.25
  109.2 17.6 %reduce-scatter.9.cloned.1.call-done = f32[128,128]{1,0:T(8,128)} async-done(((f32[512,128]{1,0:T(8,128)}), f32[128,128]{1,0:T(8,128)}) %reduce-scatter.9.cloned.1.call-update) | async-done | bytes 65552 | tf_op jit(solution)/shard_map/reduce_scatter | solution.py:106
  126.8 0.0 reduce-scatter.11.cloned.1.call-update
  126.8 0.0 reduce-scatter.7.cloned.1.call-start
  126.9 27.9 %reduce-scatter.5.cloned.1.call-done = f32[256,128]{1,0:T(8,128)} async-done(((f32[1024,128]{1,0:T(8,128)}), f32[256,128]{1,0:T(8,128)}) %reduce-scatter.5.cloned.1.call-update) | async-done | bytes 131088 | tf_op jit(solution)/shard_map/reduce_scatter | solution.py:105
  154.8 0.3 convolution_bitcast_fusion.1
  155.1 40.2 %all-reduce.2 = (f32[]{:T(128)}, f32[128]{0:T(128)}, f32[128]{0:T(128)}, f32[128,64]{0,1:T(8,128)}) all-reduce(f32[]{:T(128)} %get-tuple-element.58, f32[128]{0:T(128)S(1)} %get-tuple-element.52, f32[128]{0:T(128)S(1)} %get-tuple-element.54, f32[128,64]{0,1:T(8,128)S(1)} %convolution_bitcast_fusion.1), channel_id=1, replica_groups=mesh['row'=4,'col'=8] {'row','col'}, use_global_device_ids=true, to_apply=%region_6.7 | all-reduce | flops 8449 | bytes 67592 | tf_op jit(solution)/shard_map/psum | solution.py:112
  196.6 0.7 add_bitcast_fusion
  197.4 22.2 %reduce-scatter.7.cloned.1.call-done = f32[32,128]{1,0:T(8,128)} async-done(((f32[256,128]{1,0:T(8,128)}), f32[32,128]{1,0:T(8,128)}) %reduce-scatter.7.cloned.1.call-update) | async-done | bytes 16400 | tf_op jit(solution)/shard_map/reduce_scatter | solution.py:109
  (27 shorter events, 0.2 us)
Async XLA Ops:
  7.2 1.4 copy-start
  7.2 1.1 copy-start.1
  8.6 0.7 copy-start.3
  8.6 0.7 copy-start.6
  9.2 0.9 copy-start.7
  10.2 0.8 copy-start.2
  31.5 3.5 %copy-start.4 = (s32[16,8]{0,1:T(8,128)S(1)}, s32[16,8]{0,1:T(8,128)}, u32[]{:S(2)}) copy-start(s32[16,8]{0,1:T(8,128)} %param.14) | copy-start | bytes 1540
  31.5 8.1 %all-to-all-start.2 = ((f32[4,2,2,512]{3,2,1,0:T(2,128)}), f32[4,2,2,512]{3,2,1,0:T(2,128)S(1)}, u32[]{:S(2)}, u32[]{:S(2)}) async-start(f32[4,2,2,512]{3,2,1,0:T(2,128)} %bitcast.7), calls=%async_computation.2 | async-start | bytes 65536 | tf_op jit(solution)/shard_map/all_to_all | solution.py:55
  34.9 0.7 copy-start.5
  34.9 91.8 %reduce-scatter.9.cloned.1.call-start = ((), (), s32[]{:S(2)}) async-start(), calls=%async_computation.12 | async-start | bytes 327680 | tf_op jit(solution)/shard_map/reduce_scatter | solution.py:106
  105.8 49.0 %reduce-scatter.5.cloned.1.call-start = ((), (), s32[]{:S(2)}) async-start(), calls=%async_computation.10 | async-start | bytes 655360 | tf_op jit(solution)/shard_map/reduce_scatter | solution.py:105
  108.2 89.2 %reduce-scatter.11.cloned.1.call-start = ((), (), s32[]{:S(2)}) async-start(), calls=%async_computation.13 | async-start | bytes 73728 | tf_op jit(solution)/shard_map/reduce_scatter | solution.py:110
  126.8 92.8 %reduce-scatter.7.cloned.1.call-start = ((), (), s32[]{:S(2)}) async-start(), calls=%async_computation.11 | async-start | bytes 147456 | tf_op jit(solution)/shard_map/reduce_scatter | solution.py:109
Sparse Core Ops, SparseCore 0:
  105.9 20.8 reduce-scatter.8
  129.6 25.1 reduce-scatter.4
  157.6 30.5 reduce-scatter.10
  190.8 28.7 reduce-scatter.6
where the time goes:
time: 228 us; the launch traced here: 227 us
  blocking collectives  123 us (54%)
  waiting for transfers between devices  71.8 us (31%)
  between operations  17.2 us (8%)
  matrix products  6.04 us (3%)
  starting transfers between devices  3.56 us (2%)
  other arithmetic  3.27 us (1%)
  local copies, waits for them, and re-layouts  2.58 us (1%)
    psum x1, blocking collectives, on_device(): lax.psum((local_loss, g_gain, g_bias, grad_pde), ('row', 'col'))  40.2 us
    psum x1, blocking collectives, on_device(): valid_count = lax.psum(local_count, ('row', 'col'))  38.5 us
    reduce_scatter x1, waiting for transfers between devices, on_device(): lax.psum_scatter(g_in, 'row', scatter_dimension=0, tiled=True)  27.9 us
    reduce_scatter x1, waiting for transfers between devices, on_device(): lax.psum_scatter(row_in, 'col', scatter_dimension=0, tiled=True)  22.2 us
    all_to_all x2, blocking collectives, mirror(): lax.all_to_all(lax.all_to_all(pieces, 'row', split_axis=1, concat_axis=0,...  18.9 us
    all_to_all x2, blocking collectives, mirror(): lax.all_to_all(pieces, 'row', split_axis=1, concat_axis=0, tiled=True)  18.1 us
    reduce_scatter x1, waiting for transfers between devices, on_device(): lax.psum_scatter(g_out, 'row', scatter_dimension=0, tiled=True)  17.6 us
    all_to_all x1, blocking collectives, mirror(): lax.all_to_all(pieces, 'row', split_axis=0, concat_axis=2, tiled=True)  7.1 us
  transfers between devices with their start and end apart: 5, of which 4 were waited for; matrix products, arithmetic and copies ran while one was open for 2% of the time, Pallas kernels for 0%

commit v1 on v0

--- a/solution.py
+++ b/solution.py
@@ -4,6 +4,28 @@
 from jax.sharding import PartitionSpec as P
 
 epsilon = 1e-05
+
+
+def cut_along(shard, dim, size):
+    before, after = (shard.shape[:dim], shard.shape[dim + 1 :])
+    return jnp.moveaxis(shard.reshape(*before, size, -1, *after), dim, 0)
+
+
+def in_order(parts, dim):
+    shape = list(parts.shape[1:])
+    shape[dim] *= parts.shape[0]
+    return jnp.moveaxis(parts, 0, dim).reshape(shape)
+
+
+def exchange_directly(value, axis, split_dim, concat_dim):
+    size, index = (lax.axis_size(axis), lax.axis_index(axis))
+    blocks = cut_along(value, split_dim, size)
+    done = [blocks[index]]
+    for step in range(1, size):
+        sent = blocks[(index + step) % size]
+        done.append(lax.ppermute(sent, axis, [(i, (i + step) % size) for i in range(size)]))
+    blocks = jnp.stack(done)[(index - jnp.arange(size)) % size]
+    return in_order(blocks, concat_dim)
 
 
 def transition(rows_block, ln_gain, ln_bias, w_in, w_out):
@@ -45,11 +67,7 @@
     slab_rows = tile_cols // row_devices
     pieces = tile.reshape(factor, row_devices, slab_rows, tile_cols * channels)
     pieces = lax.all_to_all(
-        lax.all_to_all(pieces, "row", split_axis=1, concat_axis=0, tiled=True),
-        "col",
-        split_axis=0,
-        concat_axis=0,
-        tiled=True,
+        exchange_directly(pieces, "row", 1, 0), "col", split_axis=0, concat_axis=0, tiled=True
     )
     pieces = pieces.reshape(row_devices, factor, slab_rows, tile_cols * channels)
     pieces = lax.all_to_all(pieces, "row", split_axis=0, concat_axis=2, tiled=True)

time: 228 us -> 229 us (level)
  blocking collectives: 123 us -> 105 us
  starting transfers between devices: 3.56 us -> 13.2 us
  waiting for transfers between devices: 71.8 us -> 79.5 us
    all_to_all x4 -> x2, blocking collectives: 37 us -> 18.9 us  [mirror(): lax.all_to_all(exchange_directly(pieces, 'row', 1, 0), 'col', split_axis=...]
    ppermute x0 -> x6, starting transfers between devices: none -> 9.62 us  [exchange_directly(): lax.ppermute(sent, axis, [(i, (i + step) % size) for i in range(size)])]
    ppermute x0 -> x6, waiting for transfers between devices: none -> 7.72 us  [exchange_directly(): lax.ppermute(sent, axis, [(i, (i + step) % size) for i in range(size)])]
  transfers between devices with their start and end apart: 5 -> 11, of which waited for: 4 -> 9; matrix products, arithmetic and copies ran while one was open for 2% -> 2% of each run, Pallas kernels for 0% -> 0%
where the time goes in v1:
time: 229 us; the launch traced here: 228 us
  blocking collectives  105 us (46%)
  waiting for transfers between devices  79.5 us (35%)
  between operations  17.2 us (8%)
  starting transfers between devices  13.2 us (6%)
  matrix products  6.04 us (3%)
  local copies, waits for them, and re-layouts  4.63 us (2%)
  other arithmetic  2.42 us (1%)
    psum x1, blocking collectives, on_device(): lax.psum((local_loss, g_gain, g_bias, grad_pde), ('row', 'col'))  40.2 us
    psum x1, blocking collectives, on_device(): valid_count = lax.psum(local_count, ('row', 'col'))  38.5 us
    reduce_scatter x1, waiting for transfers between devices, on_device(): lax.psum_scatter(g_in, 'row', scatter_dimension=0, tiled=True)  27.9 us
    reduce_scatter x1, waiting for transfers between devices, on_device(): lax.psum_scatter(row_in, 'col', scatter_dimension=0, tiled=True)  22.2 us
    all_to_all x2, blocking collectives, mirror(): lax.all_to_all(exchange_directly(pieces, 'row', 1, 0), 'col', split_axis=...  18.9 us
    reduce_scatter x1, waiting for transfers between devices, on_device(): lax.psum_scatter(g_out, 'row', scatter_dimension=0, tiled=True)  17.6 us
    ppermute x6, starting transfers between devices, exchange_directly(): lax.ppermute(sent, axis, [(i, (i + step) % size) for i in range(size)])  9.62 us
    ppermute x6, waiting for transfers between devices, exchange_directly(): lax.ppermute(sent, axis, [(i, (i + step) % size) for i in range(size)])  7.72 us
  transfers between devices with their start and end apart: 11, of which 9 were waited for; matrix products, arithmetic and copies ran while one was open for 2% of the time, Pallas kernels for 0%

profile of v1, /device:TPU:0, one launch (start us, length us, event | category | flops | bytes accessed | tf_op | source)
XLA Modules:
  0.0 227.7 jit_solution(12321743313024409734)
XLA Ops:
  7.2 0.8 copy-done.1
  8.3 0.2 multiply_reduce_fusion.2
  8.6 0.6 copy-done.3
  9.2 0.6 fusion.8
  9.8 0.3 copy-done.7
  10.2 0.4 fusion
  10.6 0.3 copy-done.2
  10.9 0.2 fusion.10
  11.1 0.1 reshape_reshape.6
  11.3 4.0 %collective-permute-start.2 = (f32[2,1,2,512]{3,2,0,1:T(2,128)S(1)}, f32[2,1,2,512]{3,2,0,1:T(2,128)S(1)}, u32[]{:S(2)}, u32[]{:S(2)}) collective-permute-start(f32[2,1,2,512]{3,2,0,1:T(2,128)S(1)} %get-tuple-element.86), channel_id=1, source_target_pairs={{0,24},{8,0},{16,8},{24,16},{1,25},{9,1},{17,9},{25,17},{2,26},{10... | collective-permute-start | bytes 24584 | tf_op jit(solution)/shard_map/ppermute | solution.py:26
  15.2 0.5 collective-permute-start.1
  15.7 0.6 collective-permute-start
  16.4 0.2 collective-permute-done.2
  16.6 2.3 %collective-permute-done.1 = f32[2,1,2,512]{3,2,0,1:T(2,128)S(1)} collective-permute-done((f32[2,1,2,512]{3,2,0,1:T(2,128)S(1)}, f32[2,1,2,512]{3,2,0,1:T(2,128)S(1)}, u32[]{:S(2)}, u32[]{:S(2)}) %collective-permute-start.1) | collective-permute-done | bytes 8224 | tf_op jit(solution)/shard_map/ppermute | solution.py:26
  18.9 1.4 collective-permute-done
  20.3 0.6 gather_fusion
  20.9 10.5 %all_to_all.40 = f32[8,1,2,512]{3,2,1,0:T(2,128)} all-to-all(f32[8,1,2,512]{3,2,1,0:T(2,128)S(1)} %bitcast.87), channel_id=1, replica_groups=mesh['row'=4,'col'=8] {'col'}, dimensions={0} | all-to-all | bytes 65536 | tf_op jit(solution)/shard_map/all_to_all | solution.py:69
  31.4 3.4 %all-to-all-start.1 = ((f32[4,2,2,512]{3,2,1,0:T(2,128)}), f32[4,2,2,512]{3,2,1,0:T(2,128)S(1)}, u32[]{:S(2)}, u32[]{:S(2)}) async-start(f32[4,2,2,512]{3,2,1,0:T(2,128)} %bitcast.13), calls=%async_computation.1 | async-start | bytes 65536 | tf_op jit(solution)/shard_map/all_to_all | solution.py:73
  35.0 0.5 copy-done.5
  35.6 4.0 %all-to-all-done.1 = f32[4,2,2,512]{3,2,1,0:T(2,128)S(1)} async-done(((f32[4,2,2,512]{3,2,1,0:T(2,128)}), f32[4,2,2,512]{3,2,1,0:T(2,128)S(1)}, u32[]{:S(2)}, u32[]{:S(2)}) %all-to-all-start.1) | async-done | bytes 32800 | tf_op jit(solution)/shard_map/all_to_all | solution.py:73
  39.6 0.1 reshape.183
  39.8 0.2 fusion.7
  40.0 0.6 convert_reduce_fusion
  40.6 38.5 %psum.36 = f32[]{:T(128)} all-reduce(f32[]{:T(128)} %get-tuple-element.57), channel_id=1, replica_groups=mesh['row'=4,'col'=8] {'row','col'}, use_global_device_ids=true, to_apply=%region_8.9 | all-reduce | flops 1 | bytes 8 | tf_op jit(solution)/shard_map/psum | solution.py:89
  79.8 0.1 multiply_multiply_fusion
  79.9 0.1 reshape_reshape.7
  80.0 2.6 %collective-permute-start.5 = (f32[2,1,2,512]{3,2,0,1:T(2,128)S(1)}, f32[2,1,2,512]{3,2,0,1:T(2,128)S(1)}, u32[]{:S(2)}, u32[]{:S(2)}) collective-permute-start(f32[2,1,2,512]{3,2,0,1:T(2,128)S(1)} %get-tuple-element.82), channel_id=1, source_target_pairs={{0,24},{8,0},{16,8},{24,16},{1,25},{9,1},{17,9},{25,17},{2,26},{10... | collective-permute-start | bytes 24584 | tf_op jit(solution)/shard_map/ppermute | solution.py:26
  82.7 1.2 collective-permute-start.4
  83.8 0.8 collective-permute-start.3
  84.6 1.7 collective-permute-done.4
  86.3 2.1 collective-permute-done.3
  88.4 0.6 gather_fusion.1
  89.0 8.4 %all_to_all.41 = f32[8,1,2,512]{3,2,1,0:T(2,128)S(1)} all-to-all(f32[8,1,2,512]{3,2,1,0:T(2,128)S(1)} %bitcast.86), channel_id=1, replica_groups=mesh['row'=4,'col'=8] {'col'}, dimensions={0} | all-to-all | bytes 65536 | tf_op jit(solution)/shard_map/all_to_all | solution.py:69
  97.4 7.1 %all_to_all.42 = f32[4,2,2,512]{3,2,1,0:T(2,128)S(1)} all-to-all(f32[4,2,2,512]{3,2,1,0:T(2,128)S(1)} %bitcast.88), channel_id=1, replica_groups=mesh['row'=4,'col'=8] {'row'}, dimensions={0} | all-to-all | bytes 65536 | tf_op jit(solution)/shard_map/all_to_all | solution.py:73
  104.5 0.1 reshape.187
  104.6 0.1 bitcast_add_fusion
  104.7 0.2 convolution_bitcast_fusion
  104.9 1.3 fusion.6
  106.3 0.4 fusion.25
  106.8 1.8 fusion.1
  108.7 0.7 multiply_reduce_fusion
  109.4 0.2 fusion.27
  109.6 17.6 %reduce-scatter.9.cloned.1.call-done = f32[128,128]{1,0:T(8,128)} async-done(((f32[512,128]{1,0:T(8,128)}), f32[128,128]{1,0:T(8,128)}) %reduce-scatter.9.cloned.1.call-update) | async-done | bytes 65552 | tf_op jit(solution)/shard_map/reduce_scatter | solution.py:124
  127.3 27.9 %reduce-scatter.5.cloned.1.call-done = f32[256,128]{1,0:T(8,128)} async-done(((f32[1024,128]{1,0:T(8,128)}), f32[256,128]{1,0:T(8,128)}) %reduce-scatter.5.cloned.1.call-update) | async-done | bytes 131088 | tf_op jit(solution)/shard_map/reduce_scatter | solution.py:123
  155.3 0.3 convolution_bitcast_fusion.1
  155.5 40.2 %all-reduce.2 = (f32[]{:T(128)}, f32[128]{0:T(128)}, f32[128]{0:T(128)}, f32[128,64]{0,1:T(8,128)}) all-reduce(f32[]{:T(128)} %get-tuple-element.58, f32[128]{0:T(128)S(1)} %get-tuple-element.52, f32[128]{0:T(128)S(1)} %get-tuple-element.54, f32[128,64]{0,1:T(8,128)S(1)} %convolution_bitcast_fusion.1), channel_id=1, replica_groups=mesh['row'=4,'col'=8] {'row','col'}, use_global_device_ids=true, to_apply=%region_6.7 | all-reduce | flops 8449 | bytes 67592 | tf_op jit(solution)/shard_map/psum | solution.py:130
  197.1 0.7 add_bitcast_fusion
  197.8 22.2 %reduce-scatter.7.cloned.1.call-done = f32[32,128]{1,0:T(8,128)} async-done(((f32[256,128]{1,0:T(8,128)}), f32[32,128]{1,0:T(8,128)}) %reduce-scatter.7.cloned.1.call-update) | async-done | bytes 16400 | tf_op jit(solution)/shard_map/reduce_scatter | solution.py:127
  (43 shorter events, 0.9 us)
Async XLA Ops:
  7.2 1.4 copy-start
  7.2 0.9 copy-start.1
  8.5 0.7 copy-start.3
  8.5 0.7 copy-start.6
  9.2 0.9 copy-start.7
  10.2 0.8 copy-start.2
  11.3 5.3 %collective-permute-start.2 = (f32[2,1,2,512]{3,2,0,1:T(2,128)S(1)}, f32[2,1,2,512]{3,2,0,1:T(2,128)S(1)}, u32[]{:S(2)}, u32[]{:S(2)}) collective-permute-start(f32[2,1,2,512]{3,2,0,1:T(2,128)S(1)} %get-tuple-element.86), channel_id=1, source_target_pairs={{0,24},{8,0},{16,8},{24,16},{1,25},{9,1},{17,9},{25,17},{2,26},{10... | collective-permute-start | bytes 24584 | tf_op jit(solution)/shard_map/ppermute | solution.py:26
  15.2 3.7 %collective-permute-start.1 = (f32[2,1,2,512]{3,2,0,1:T(2,128)S(1)}, f32[2,1,2,512]{3,2,0,1:T(2,128)S(1)}, u32[]{:S(2)}, u32[]{:S(2)}) collective-permute-start(f32[2,1,2,512]{3,2,0,1:T(2,128)S(1)} %get-tuple-element.87), channel_id=1, source_target_pairs={{0,16},{8,24},{16,0},{24,8},{1,17},{9,25},{17,1},{25,9},{2,18},{10... | collective-permute-start | bytes 24584 | tf_op jit(solution)/shard_map/ppermute | solution.py:26
  15.7 4.5 %collective-permute-start = (f32[2,1,2,512]{3,2,0,1:T(2,128)S(1)}, f32[2,1,2,512]{3,2,0,1:T(2,128)S(1)}, u32[]{:S(2)}, u32[]{:S(2)}) collective-permute-start(f32[2,1,2,512]{3,2,0,1:T(2,128)S(1)} %get-tuple-element.88), channel_id=1, source_target_pairs={{0,8},{8,16},{16,24},{24,0},{1,9},{9,17},{17,25},{25,1},{2,10},{10... | collective-permute-start | bytes 24584 | tf_op jit(solution)/shard_map/ppermute | solution.py:26
  31.4 3.5 %copy-start.4 = (s32[16,8]{0,1:T(8,128)S(1)}, s32[16,8]{0,1:T(8,128)}, u32[]{:S(2)}) copy-start(s32[16,8]{0,1:T(8,128)} %param.14) | copy-start | bytes 1540
  31.4 8.1 %all-to-all-start.1 = ((f32[4,2,2,512]{3,2,1,0:T(2,128)}), f32[4,2,2,512]{3,2,1,0:T(2,128)S(1)}, u32[]{:S(2)}, u32[]{:S(2)}) async-start(f32[4,2,2,512]{3,2,1,0:T(2,128)} %bitcast.13), calls=%async_computation.1 | async-start | bytes 65536 | tf_op jit(solution)/shard_map/all_to_all | solution.py:73
  34.8 0.7 copy-start.5
  34.8 92.4 %reduce-scatter.9.cloned.1.call-start = ((), (), s32[]{:S(2)}) async-start(), calls=%async_computation.10 | async-start | bytes 327680 | tf_op jit(solution)/shard_map/reduce_scatter | solution.py:124
  80.0 4.5 %collective-permute-start.5 = (f32[2,1,2,512]{3,2,0,1:T(2,128)S(1)}, f32[2,1,2,512]{3,2,0,1:T(2,128)S(1)}, u32[]{:S(2)}, u32[]{:S(2)}) collective-permute-start(f32[2,1,2,512]{3,2,0,1:T(2,128)S(1)} %get-tuple-element.82), channel_id=1, source_target_pairs={{0,24},{8,0},{16,8},{24,16},{1,25},{9,1},{17,9},{25,17},{2,26},{10... | collective-permute-start | bytes 24584 | tf_op jit(solution)/shard_map/ppermute | solution.py:26
  82.7 3.7 %collective-permute-start.4 = (f32[2,1,2,512]{3,2,0,1:T(2,128)S(1)}, f32[2,1,2,512]{3,2,0,1:T(2,128)S(1)}, u32[]{:S(2)}, u32[]{:S(2)}) collective-permute-start(f32[2,1,2,512]{3,2,0,1:T(2,128)S(1)} %get-tuple-element.83), channel_id=1, source_target_pairs={{0,16},{8,24},{16,0},{24,8},{1,17},{9,25},{17,1},{25,9},{2,18},{10... | collective-permute-start | bytes 24584 | tf_op jit(solution)/shard_map/ppermute | solution.py:26
  83.8 4.5 %collective-permute-start.3 = (f32[2,1,2,512]{3,2,0,1:T(2,128)S(1)}, f32[2,1,2,512]{3,2,0,1:T(2,128)S(1)}, u32[]{:S(2)}, u32[]{:S(2)}) collective-permute-start(f32[2,1,2,512]{3,2,0,1:T(2,128)S(1)} %get-tuple-element.84), channel_id=1, source_target_pairs={{0,8},{8,16},{16,24},{24,0},{1,9},{9,17},{17,25},{25,1},{2,10},{10... | collective-permute-start | bytes 24584 | tf_op jit(solution)/shard_map/ppermute | solution.py:26
  106.3 49.0 %reduce-scatter.5.cloned.1.call-start = ((), (), s32[]{:S(2)}) async-start(), calls=%async_computation.8 | async-start | bytes 655360 | tf_op jit(solution)/shard_map/reduce_scatter | solution.py:123
  108.6 89.2 %reduce-scatter.11.cloned.1.call-start = ((), (), s32[]{:S(2)}) async-start(), calls=%async_computation.11 | async-start | bytes 73728 | tf_op jit(solution)/shard_map/reduce_scatter | solution.py:128
  127.3 92.8 %reduce-scatter.7.cloned.1.call-start = ((), (), s32[]{:S(2)}) async-start(), calls=%async_computation.9 | async-start | bytes 147456 | tf_op jit(solution)/shard_map/reduce_scatter | solution.py:127
Sparse Core Ops, SparseCore 0:
  106.4 20.8 reduce-scatter.8
  130.1 25.1 reduce-scatter.4
  158.1 30.5 reduce-scatter.10
  191.3 28.7 reduce-scatter.6
